TPU v7x, 128 devices: a whole 4x4x4 slice. The times are simulated.
128 devices in a mesh: group: 8 (over y, core), within: 16 (over z, x).
Axes of the slice: x: 4, y: 4, z: 4, core: 2. Of those that a mesh axis runs over, the one named last changes fastest.
Arguments:
- tokens: bfloat16 [16384, 2048], P(('group', 'within')), may hold values from -6 to 6
- languages: int32 [16384], P(('group', 'within')), may hold values from 0 to 99, as said below
- lang_group: int32 [100], replicated, may hold values from 0 to 7, as said below
- group_gain: float32 [8, 2048], replicated, may hold values from 0.25 to 1.75
- group_w1: bfloat16 [8, 2048, 8192], P('group', None, 'within'), may hold values from -0.125 to 0.125
- group_b1: float32 [8, 8192], P('group', 'within'), may hold values from -3 to 3
- group_w2: bfloat16 [8, 8192, 2048], P('group', 'within'), may hold values from -0.0625 to 0.0625
- group_b2: float32 [8, 2048], replicated, may hold values from -3 to 3
- shared_gain: float32 [2048], replicated, may hold values from 0.25 to 1.75
- shared_w1: bfloat16 [2048, 8192], P(None, 'group'), may hold values from -0.125 to 0.125
- shared_b1: float32 [8192], P('group'), may hold values from -3 to 3
- shared_w2: bfloat16 [8192, 2048], P('group'), may hold values from -0.0625 to 0.0625
- shared_b2: float32 [2048], replicated, may hold values from -3 to 3
Outputs:
- encoded: bfloat16 [16384, 2048], P(('group', 'within'))
Inputs may be any that keep to these rules, and one draw needn't show every extreme that they name: `lang_group`: every language lies in one group and every group holds at least one language. Among the 128 tokens of one device (an aligned block), at most 24 have languages of one group, and in every block some group has exactly 24.
All inputs are finite; a program needn't handle non-finite values.
Results may differ from a plain program's by a relative error of at most 0.017.
Values may be sent and summed in bfloat16 or wider, within the bound.
No kernel may reach another device: no remote copies, remote signals or barrier semaphores. Data moves between devices by JAX's collectives and lax.ppermute only.
A program may use at most 128 MiB of HBM per device.

v0:
```python
import jax
import jax.numpy as jnp
from jax import lax
from jax.sharding import PartitionSpec as P


def layer_norm(values, gains):
    centre = jnp.mean(values, axis=-1, keepdims=True)
    centred = values - centre
    spread = jnp.mean(centred * centred, axis=-1, keepdims=True)
    return centred * lax.rsqrt(spread + 1e-05) * gains


def on_device(
    tokens,
    languages,
    lang_group,
    group_gain,
    group_w1,
    group_b1,
    group_w2,
    group_b2,
    shared_gain,
    shared_w1,
    shared_b1,
    shared_w2,
    shared_b2,
):
    tok_dev = tokens.shape[0]
    width_model = tokens.shape[1]
    num_groups = group_gain.shape[0]
    num_langs = lang_group.shape[0]
    capacity = 3 * tok_dev // (2 * lax.axis_size("group"))
    residual_in = tokens.astype(jnp.float32)
    lang_hit = (languages[:, None] == jnp.arange(num_langs, dtype=jnp.int32)[None, :]).astype(
        jnp.int32
    )
    group_of = jnp.sum(lang_hit * lang_group[None, :], axis=1)
    onehot = (group_of[:, None] == jnp.arange(num_groups, dtype=jnp.int32)[None, :]).astype(
        jnp.int32
    )
    earlier = jnp.cumsum(onehot, axis=0) - onehot
    slot_index = jnp.sum(earlier * onehot, axis=1)
    position = group_of * capacity + slot_index
    dispatch_map = (
        position[None, :] == jnp.arange(num_groups * capacity, dtype=jnp.int32)[:, None]
    ).astype(jnp.bfloat16)
    onehot_float = onehot.astype(jnp.float32)
    row_gains = jnp.dot(onehot_float, group_gain, precision=lax.Precision.HIGHEST)
    normed = layer_norm(residual_in, row_gains).astype(jnp.bfloat16)
    outgoing = jnp.dot(dispatch_map, normed, preferred_element_type=jnp.float32).astype(
        jnp.bfloat16
    )
    outgoing = outgoing.reshape(num_groups, capacity, width_model)
    arrived = lax.all_to_all(outgoing, "group", split_axis=0, concat_axis=0, tiled=True)
    group_rows = arrived.reshape(num_groups * capacity, width_model)
    first_proj = group_w1[0]
    first_bias = group_b1[0]
    second_proj = group_w2[0]
    hidden = jax.nn.relu(
        jnp.dot(
            lax.all_gather(group_rows, "within", axis=0, tiled=True),
            first_proj,
            preferred_element_type=jnp.float32,
        )
        + first_bias
    ).astype(jnp.bfloat16)
    selected = hidden
    summed = lax.psum_scatter(
        jnp.dot(selected, second_proj, preferred_element_type=jnp.float32).astype(jnp.bfloat16),
        "within",
        scatter_dimension=0,
        tiled=True,
    )
    returned = lax.all_to_all(
        summed.reshape(num_groups, capacity, width_model),
        "group",
        split_axis=0,
        concat_axis=0,
        tiled=True,
    )
    returned = returned.reshape(num_groups * capacity, width_model)
    group_out = lax.dot_general(
        dispatch_map, returned, (((0,), (0,)), ((), ())), preferred_element_type=jnp.float32
    )
    group_bias = jnp.dot(onehot_float, group_b2, precision=lax.Precision.HIGHEST)
    middle = residual_in + group_out + group_bias
    shared_in = layer_norm(middle, shared_gain).astype(jnp.bfloat16)
    shared_hidden = jax.nn.relu(
        jnp.dot(
            lax.all_gather(shared_in, "group", axis=0, tiled=True),
            shared_w1,
            preferred_element_type=jnp.float32,
        )
        + shared_b1
    ).astype(jnp.bfloat16)
    selected = shared_hidden
    shared_out = lax.psum_scatter(
        jnp.dot(selected, shared_w2, preferred_element_type=jnp.float32).astype(jnp.bfloat16),
        "group",
        scatter_dimension=0,
        tiled=True,
    ).astype(jnp.float32)
    return (middle + shared_out + shared_b2).astype(jnp.bfloat16)


def solution(mesh):
    placed = (
        P(("group", "within"), None),
        P(("group", "within")),
        P(),
        P(),
        P("group", None, "within"),
        P("group", "within"),
        P("group", "within", None),
        P(),
        P(),
        P(None, "group"),
        P("group"),
        P("group", None),
        P(),
    )
    return jax.shard_map(
        on_device,
        mesh=mesh,
        in_specs=placed,
        out_specs=P(("group", "within"), None),
        check_vma=False,
    )
```

profile of v0, /device:TPU:0, one launch (start us, length us, event | category | flops | bytes accessed | tf_op | source)
XLA Modules:
  0.0 346.0 jit_solution(16796450870467543149)
XLA Ops:
  6.5 0.0 copy-start
  6.5 0.0 copy-start.6
  6.5 0.0 all-gather.3.cloned.1.call-start
  6.5 1.3 convert_reduce_fusion
  7.9 1.3 fusion.10
  9.2 0.8 select_reduce_fusion
  10.0 0.1 fusion.17
  10.1 0.2 reduce_window_sum.11
  10.3 0.2 fusion.16
  10.5 2.2 fusion
  12.6 0.4 convolution_convert_fusion.2
  13.0 17.7 %all_to_all.10 = bf16[8,24,2048]{2,1,0:T(8,128)(2,1)} all-to-all(bf16[8,24,2048]{2,1,0:T(8,128)(2,1)S(1)} %bitcast.22), channel_id=1, replica_groups=mesh['group'=8,'within'=16] {'group'}, dimensions={0} | all-to-all | bytes 1572864 | tf_op jit(solution)/shard_map/all_to_all | solution.py:55
  30.7 0.0 all-gather.3.cloned.1.call-update
  30.7 0.0 reduce-scatter.3.cloned.1.call-start
  30.8 90.6 %all-gather.3.cloned.1.call-done = bf16[3072,2048]{1,0:T(8,128)(2,1)} async-done(((bf16[192,2048]{1,0:T(8,128)(2,1)}), bf16[3072,2048]{1,0:T(8,128)(2,1)}) %all-gather.3.cloned.1.call-update) | async-done | bytes 12582928 | tf_op jit(solution)/shard_map/all_gather | solution.py:62
  121.4 0.0 copy-done
  121.4 0.0 copy-done.6
  121.4 19.5 %convolution_convert_fusion = bf16[3072,2048]{1,0:T(8,128)(2,1)} fusion(bf16[1,512,2048]{2,1,0:T(8,128)(2,1)S(1)} %copy-done, bf16[3072,2048]{1,0:T(8,128)(2,1)} %all-gather.3.cloned.1.call-done, f32[512]{0:T(512)S(1)} %bitcast.24, bf16[1,2048,512]{2,1,0:T(8,128)(2,1)} %param.17), kind=kOutput, calls=%fused_computation | convolution fusion | flops 12895911936 | bytes 29362176 | tf_op jit(solution)/shard_map/dot_general | solution.py:70
  140.8 0.0 copy-start.1
  140.8 0.0 copy-start.2
  140.8 0.0 reduce-scatter.3.cloned.1.call-update
  140.9 0.0 copy-start.3
  140.9 0.0 all-gather.5.cloned.1.call-start
  140.9 94.3 %reduce-scatter.3.cloned.1.call-done = bf16[192,2048]{1,0:T(8,128)(2,1)} async-done(((bf16[3072,2048]{1,0:T(8,128)(2,1)}), bf16[192,2048]{1,0:T(8,128)(2,1)}) %reduce-scatter.3.cloned.1.call-update) | async-done | bytes 786448 | tf_op jit(solution)/shard_map/reduce_scatter | solution.py:69
  235.2 17.5 %all_to_all.11 = bf16[8,24,2048]{2,1,0:T(8,128)(2,1)S(1)} all-to-all(bf16[8,24,2048]{2,1,0:T(8,128)(2,1)} %bitcast.23), channel_id=1, replica_groups=mesh['group'=8,'within'=16] {'group'}, dimensions={0} | all-to-all | bytes 1572864 | tf_op jit(solution)/shard_map/all_to_all | solution.py:75
  252.7 0.0 copy-start.5
  252.7 0.0 copy-done.1
  252.7 0.4 convolution_add_fusion.1
  253.1 0.0 copy-done.2
  253.1 1.1 fusion.24
  254.3 0.3 multiply_reduce_fusion
  254.5 0.0 copy-done.3
  254.5 1.0 multiply_convert_fusion
  255.5 0.0 all-gather.5.cloned.1.call-update
  255.6 0.2 reduce-scatter.5.cloned.1.call-start
  255.8 29.2 %all-gather.5.cloned.1.call-done = bf16[1024,2048]{1,0:T(8,128)(2,1)} async-done(((bf16[128,2048]{1,0:T(8,128)(2,1)}), bf16[1024,2048]{1,0:T(8,128)(2,1)}) %all-gather.5.cloned.1.call-update) | async-done | bytes 4194320 | tf_op jit(solution)/shard_map/all_gather | solution.py:91
  285.0 0.0 copy-done.5
  285.0 14.3 %convolution_convert_fusion.1 = bf16[1024,2048]{1,0:T(8,128)(2,1)} fusion(bf16[1024,2048]{1,0:T(8,128)(2,1)} %param.24, f32[1024]{0:T(1024)S(1)} %copy-done.5, bf16[1024,2048]{1,0:T(8,128)(2,1)} %all-gather.5.cloned.1.call-done, bf16[2048,1024]{1,0:T(8,128)(2,1)} %param.22), kind=kOutput, calls=%fused_computation.3 | convolution fusion | flops 8595177472 | bytes 16781312 | tf_op jit(solution)/shard_map/dot_general | solution.py:99
  299.3 0.0 copy-start.4
  299.3 0.0 reduce-scatter.5.cloned.1.call-update
  299.4 38.1 %reduce-scatter.5.cloned.1.call-done = bf16[128,2048]{1,0:T(8,128)(2,1)} async-done(((bf16[1024,2048]{1,0:T(8,128)(2,1)}), bf16[128,2048]{1,0:T(8,128)(2,1)}) %reduce-scatter.5.cloned.1.call-update) | async-done | bytes 524304 | tf_op jit(solution)/shard_map/reduce_scatter | solution.py:98
  337.5 0.0 copy-done.4
  337.5 2.0 add_convert_fusion
  (5 shorter events, 0.0 us)
Async XLA Ops:
  6.5 114.8 %copy-start = (bf16[1,512,2048]{2,1,0:T(8,128)(2,1)S(1)}, bf16[1,512,2048]{2,1,0:T(8,128)(2,1)}, u32[]{:S(2)}) copy-start(bf16[1,512,2048]{2,1,0:T(8,128)(2,1)} %param.19) | copy-start | bytes 6291460
  6.5 114.8 %copy-start.6 = (f32[1,512]{1,0:T(1,128)S(1)}, f32[1,512]{1,0:T(1,128)}, u32[]{:S(2)}) copy-start(f32[1,512]{1,0:T(1,128)} %param.18) | copy-start | bytes 6148
  6.5 114.8 %all-gather.3.cloned.1.call-start = ((), (), s32[]{:S(2)}) async-start(), calls=%async_computation.4 | async-start | bytes 13369344 | tf_op jit(solution)/shard_map/all_gather | solution.py:62
  30.7 204.5 %reduce-scatter.3.cloned.1.call-start = ((), (), s32[]{:S(2)}) async-start(), calls=%async_computation.5 | async-start | bytes 13369344 | tf_op jit(solution)/shard_map/reduce_scatter | solution.py:69
  140.8 111.9 %copy-start.1 = (bf16[128,2048]{1,0:T(8,128)(2,1)S(1)}, bf16[128,2048]{1,0:T(8,128)(2,1)}, u32[]{:S(2)}) copy-start(bf16[128,2048]{1,0:T(8,128)(2,1)} %param.13) | copy-start | bytes 1572868
  140.8 112.3 %copy-start.2 = (f32[8,2048]{1,0:T(8,128)S(1)}, f32[8,2048]{1,0:T(8,128)}, u32[]{:S(2)}) copy-start(f32[8,2048]{1,0:T(8,128)} %param.20) | copy-start | bytes 196612
  140.9 113.7 %copy-start.3 = (f32[2048]{0:T(1024)S(1)}, f32[2048]{0:T(1024)}, u32[]{:S(2)}) copy-start(f32[2048]{0:T(1024)} %param.21) | copy-start | bytes 24580
  140.9 144.1 %all-gather.5.cloned.1.call-start = ((), (), s32[]{:S(2)}) async-start(), calls=%async_computation.6 | async-start | bytes 4718592 | tf_op jit(solution)/shard_map/all_gather | solution.py:91
  252.7 32.3 %copy-start.5 = (f32[1024]{0:T(1024)S(1)}, f32[1024]{0:T(1024)}, u32[]{:S(2)}) copy-start(f32[1024]{0:T(1024)} %param.23) | copy-start | bytes 12292
  255.6 81.9 %reduce-scatter.5.cloned.1.call-start = ((), (), s32[]{:S(2)}) async-start(), calls=%async_computation.7 | async-start | bytes 4718592 | tf_op jit(solution)/shard_map/reduce_scatter | solution.py:98
  299.3 38.1 %copy-start.4 = (f32[2048]{0:T(1024)S(1)}, f32[2048]{0:T(1024)}, u32[]{:S(2)}) copy-start(f32[2048]{0:T(1024)} %param.25) | copy-start | bytes 24580
Sparse Core Ops, SparseCore 0:
  30.8 90.4 all-gather.2
  141.0 94.1 reduce-scatter.2
  255.7 29.2 all-gather.4
  299.5 37.9 reduce-scatter.4
where the time goes:
time: 346 us
  waiting for transfers between devices  252 us (73%)
  matrix products  37.8 us (11%)
  blocking collectives  35.2 us (10%)
  between operations  13.2 us (4%)
  other arithmetic  7.17 us (2%)
    reduce_scatter x1, waiting for transfers between devices, on_device(): lax.psum_scatter(jnp.dot(selected, second_proj, preferred_element_type=jn...  94.3 us
    all_gather x1, waiting for transfers between devices, on_device(): lax.all_gather(group_rows, 'within', axis=0, tiled=True)  90.6 us
    reduce_scatter x1, waiting for transfers between devices, on_device(): lax.psum_scatter(jnp.dot(selected, shared_w2, preferred_element_type=jnp....  38.1 us
    all_gather x1, waiting for transfers between devices, on_device(): lax.all_gather(shared_in, 'group', axis=0, tiled=True)  29.2 us
    dot_general x1, matrix products, on_device(): jnp.dot(selected, second_proj, preferred_element_type=jnp.float32)  19.5 us
    all_to_all x1, blocking collectives, on_device(): lax.all_to_all(outgoing, 'group', split_axis=0, concat_axis=0, tiled=True)  17.7 us
    all_to_all x1, blocking collectives, on_device(): lax.all_to_all(summed.reshape(num_groups, capacity, width_model), 'group'...  17.5 us
    dot_general x1, matrix products, on_device(): jnp.dot(selected, shared_w2, preferred_element_type=jnp.float32)  14.3 us
  transfers between devices with their start and end apart: 4, of which 4 were waited for; matrix products, arithmetic and copies ran while one was open for 0% of the time, Pallas kernels for 0%

commit v1 on v0

v1 whole, which is shorter than its diff:
```python
import jax
import jax.numpy as jnp
from jax import lax
from jax.sharding import Mesh, PartitionSpec as P

X = ("xh", "xl")


def layer_norm(values, gains):
    centre = jnp.mean(values, axis=-1, keepdims=True)
    centred = values - centre
    spread = jnp.mean(centred * centred, axis=-1, keepdims=True)
    return centred * lax.rsqrt(spread + 1e-05) * gains


def shift(value, axis, step):
    size = lax.axis_size(axis)
    return lax.ppermute(value, axis, [(i, (i + step) % size) for i in range(size)])


def swap_column(value):
    return lax.ppermute(value, "xl", [(0, 1), (1, 0)])


def swap_blocks(value):
    return lax.ppermute(value, X, [(0, 3), (3, 0), (1, 2), (2, 1)])


def swap_core(value):
    return lax.ppermute(value, "core", [(0, 1), (1, 0)])


def ring_gather(rows, axis):
    half = rows.shape[0] // 2
    prev = shift(rows, axis, 1)
    foll = shift(rows, axis, -1)
    far_a = shift(prev[:half], axis, 1)
    far_b = shift(foll[half:], axis, -1)
    return rows, prev, foll, jnp.concatenate([far_a, far_b], axis=0)


def up(value):
    return value.astype(jnp.float32)


def ring_scatter(own, prev, foll, far, axis):
    half = far.shape[0] // 2
    via_prev = shift(far[:half], axis, -1)
    via_foll = shift(far[half:], axis, 1)
    prev = jnp.concatenate(
        [(up(prev[:half]) + up(via_prev)).astype(jnp.bfloat16), prev[half:]], axis=0
    )
    foll = jnp.concatenate(
        [foll[:half], (up(foll[half:]) + up(via_foll)).astype(jnp.bfloat16)], axis=0
    )
    from_foll = shift(prev, axis, -1)
    from_prev = shift(foll, axis, 1)
    return up(own) + up(from_foll) + up(from_prev)


def on_device(
    tokens,
    languages,
    lang_group,
    group_gain,
    group_w1,
    group_b1,
    group_w2,
    group_b2,
    shared_gain,
    shared_w1,
    shared_b1,
    shared_w2,
    shared_b2,
):
    tok_dev = tokens.shape[0]
    width_model = tokens.shape[1]
    num_groups = group_gain.shape[0]
    num_langs = lang_group.shape[0]
    capacity = 3 * tok_dev // (2 * num_groups)
    bf16 = jnp.bfloat16

    w1 = jnp.concatenate([group_w1[0], swap_blocks(group_w1[0])], axis=1)
    b1 = jnp.concatenate([group_b1[0], swap_blocks(group_b1[0])])
    w2 = jnp.concatenate([group_w2[0], swap_blocks(group_w2[0])], axis=0)
    sw1 = jnp.concatenate([shared_w1, swap_core(shared_w1)], axis=1)
    sb1 = jnp.concatenate([shared_b1, swap_core(shared_b1)])
    sw2 = jnp.concatenate([shared_w2, swap_core(shared_w2)], axis=0)

    residual_in = tokens.astype(jnp.float32)
    lang_hit = (languages[:, None] == jnp.arange(num_langs, dtype=jnp.int32)[None, :]).astype(
        jnp.int32
    )
    group_of = jnp.sum(lang_hit * lang_group[None, :], axis=1)
    onehot = (group_of[:, None] == jnp.arange(num_groups, dtype=jnp.int32)[None, :]).astype(
        jnp.int32
    )
    earlier = jnp.cumsum(onehot, axis=0) - onehot
    slot_index = jnp.sum(earlier * onehot, axis=1)
    position = group_of * capacity + slot_index
    dispatch_map = (
        position[None, :] == jnp.arange(num_groups * capacity, dtype=jnp.int32)[:, None]
    ).astype(bf16)
    onehot_float = onehot.astype(jnp.float32)
    row_gains = jnp.dot(onehot_float, group_gain, precision=lax.Precision.HIGHEST)
    normed = layer_norm(residual_in, row_gains).astype(bf16)
    outgoing = jnp.dot(dispatch_map, normed, preferred_element_type=jnp.float32).astype(bf16)
    outgoing = outgoing.reshape(num_groups, capacity, width_model)
    arrived = lax.all_to_all(outgoing, ("y", "core"), split_axis=0, concat_axis=0, tiled=True)
    rows = arrived.reshape(num_groups * capacity, width_model)

    cut = 7 * rows.shape[0] // 16 // 16 * 16
    part_a, part_b = rows[:cut], rows[cut:]
    size_a, size_b = part_a.shape[0], part_b.shape[0]
    pair_b = swap_column(part_b)
    a_own = jnp.concatenate(ring_gather(part_a, "z"), axis=0)
    b_all = jnp.concatenate(
        ring_gather(jnp.concatenate([part_b, pair_b], axis=0), "z"), axis=0
    )
    a_pair = swap_column(a_own)

    def feed_forward(block):
        hidden = jax.nn.relu(jnp.dot(block, w1, preferred_element_type=jnp.float32) + b1)
        return jnp.dot(hidden.astype(bf16), w2, preferred_element_type=jnp.float32)

    a_back = swap_column(feed_forward(a_pair).astype(bf16))
    b_part = feed_forward(b_all).astype(bf16)
    b_sum = ring_scatter(*jnp.split(b_part, 4), "z")
    a_part = (feed_forward(a_own) + up(a_back)).astype(bf16)
    a_sum = ring_scatter(*jnp.split(a_part, 4), "z")
    b_sum = b_sum[:size_b] + up(swap_column(b_sum[size_b:].astype(bf16)))
    summed = jnp.concatenate([a_sum, b_sum], axis=0).astype(bf16)

    returned = lax.all_to_all(
        summed.reshape(num_groups, capacity, width_model),
        ("y", "core"),
        split_axis=0,
        concat_axis=0,
        tiled=True,
    )
    returned = returned.reshape(num_groups * capacity, width_model)
    group_out = lax.dot_general(
        dispatch_map, returned, (((0,), (0,)), ((), ())), preferred_element_type=jnp.float32
    )
    group_bias = jnp.dot(onehot_float, group_b2, precision=lax.Precision.HIGHEST)
    middle = residual_in + group_out + group_bias
    shared_in = layer_norm(middle, shared_gain).astype(bf16)

    def shared_forward(block):
        hidden = jax.nn.relu(jnp.dot(block, sw1, preferred_element_type=jnp.float32) + sb1)
        return jnp.dot(hidden.astype(bf16), sw2, preferred_element_type=jnp.float32).astype(bf16)

    own, prev, foll, far = ring_gather(shared_in, "y")
    near = shared_forward(jnp.concatenate([own, prev, foll], axis=0))
    far = shared_forward(far)
    shared_out = ring_scatter(
        near[:tok_dev], near[tok_dev : 2 * tok_dev], near[2 * tok_dev :], far, "y"
    )
    return (middle + shared_out + shared_b2).astype(bf16)


def solution(mesh):
    chips = Mesh(mesh.devices.reshape(4, 2, 4, 2, 2), ("y", "core", "z", "xh", "xl"))
    group = ("y", "core")
    within = ("z", "xh", "xl")
    both = group + within
    placed = (
        P(both, None),
        P(both),
        P(),
        P(),
        P(group, None, within),
        P(group, within),
        P(group, within, None),
        P(),
        P(),
        P(None, group),
        P(group),
        P(group, None),
        P(),
    )
    return jax.shard_map(
        on_device,
        mesh=chips,
        in_specs=placed,
        out_specs=P(both, None),
        check_vma=False,
    )
```

time: 346 us -> 291 us (0.84)
  waiting for transfers between devices: 252 us -> 148 us
  starting transfers between devices: 0.31 us -> 52.4 us
  blocking collectives: 35.2 us -> 0 us
  local copies, waits for them, and re-layouts: 0.03 us -> 24.2 us
  matrix products: 37.8 us -> 54.4 us
  between operations: 13.2 us -> 0.45 us
    ppermute x0 -> x34, waiting for transfers between devices: none -> 136 us  [the longest x24 87.6 us: shift(): lax.ppermute(value, axis, [(i, (i + step) % size) for i in range(size)])]
    reduce_scatter x2 -> x0, waiting for transfers between devices: 132 us -> none  [the longest x1 94.3 us: on_device(): lax.psum_scatter(jnp.dot(selected, second_proj, preferred_element_type=jn...]
    all_gather x2 -> x0, waiting for transfers between devices: 120 us -> none  [the longest x1 90.6 us: on_device(): lax.all_gather(group_rows, 'within', axis=0, tiled=True)]
    ppermute x0 -> x34, starting transfers between devices: none -> 43.8 us  [the longest x24 32.4 us: shift(): lax.ppermute(value, axis, [(i, (i + step) % size) for i in range(size)])]
    all_to_all x2 -> x0, blocking collectives: 35.2 us -> none  [the longest x1 17.7 us: on_device(): lax.all_to_all(outgoing, 'group', split_axis=0, concat_axis=0, tiled=True)]
    dot_general x2 -> x5, matrix products: 33.8 us -> 49.5 us  [the longest x3 28.5 us: feed_forward(): return jnp.dot(hidden.astype(bf16), w2, preferred_element_type=jnp.float32)]
    all_to_all x0 -> x2, waiting for transfers between devices: none -> 12.7 us  [the longest x1 7.07 us: on_device(): lax.all_to_all(outgoing, ('y', 'core'), split_axis=0, concat_axis=0, tile...]
    unnamed x14 -> x32, local copies, waits for them, and re-layouts: 0.03 us -> 10.5 us
  transfers between devices with their start and end apart: 4 -> 36, of which waited for: 4 -> 20; matrix products, arithmetic and copies ran while one was open for 0% -> 24% of each run, Pallas kernels for 0% -> 0%
where the time goes in v1:
time: 291 us; the launch traced here: 290 us
  waiting for transfers between devices  148 us (51%)
  matrix products  54.4 us (19%)
  starting transfers between devices  52.4 us (18%)
  local copies, waits for them, and re-layouts  24.2 us (8%)
  other arithmetic  10.2 us (4%)
    ppermute x24, waiting for transfers between devices, shift(): lax.ppermute(value, axis, [(i, (i + step) % size) for i in range(size)])  87.6 us
    ppermute x24, starting transfers between devices, shift(): lax.ppermute(value, axis, [(i, (i + step) % size) for i in range(size)])  32.4 us
    ppermute x3, waiting for transfers between devices, swap_blocks(): return lax.ppermute(value, X, [(0, 3), (3, 0), (1, 2), (2, 1)])  29.8 us
    dot_general x3, matrix products, feed_forward(): return jnp.dot(hidden.astype(bf16), w2, preferred_element_type=jnp.float32)  28.5 us
    dot_general x2, matrix products, shared_forward(): jnp.dot(hidden.astype(bf16), sw2, preferred_element_type=jnp.float32)  21 us
    ppermute x4, waiting for transfers between devices, swap_column(): return lax.ppermute(value, 'xl', [(0, 1), (1, 0)])  18.2 us
    unnamed x32, local copies, waits for them, and re-layouts  10.5 us
    all_to_all x1, waiting for transfers between devices, on_device(): lax.all_to_all(outgoing, ('y', 'core'), split_axis=0, concat_axis=0, tile...  7.07 us
  transfers between devices with their start and end apart: 36, of which 20 were waited for; matrix products, arithmetic and copies ran while one was open for 24% of the time, Pallas kernels for 0%

profile of v1, /device:TPU:0, one launch (start us, length us, event | category | flops | bytes accessed | tf_op | source)
XLA Modules:
  0.0 290.0 jit_solution(11847718999028674185)
XLA Ops:
  0.0 1.2 convert_reduce_fusion
  1.3 1.3 fusion.18
  2.6 0.8 select_reduce_fusion
  3.8 2.2 fusion.2
  6.0 1.2 convolution_convert_fusion.3
  7.2 4.5 %all-to-all-start = ((bf16[8,24,2048]{2,1,0:T(8,128)(2,1)}), bf16[8,24,2048]{2,1,0:T(8,128)(2,1)S(1)}, u32[]{:S(2)}, u32[]{:S(2)}) async-start(bf16[8,24,2048]{2,1,0:T(8,128)(2,1)} %bitcast), calls=%async_computation | async-start | bytes 1572864 | tf_op jit(solution)/shard_map/all_to_all | solution.py:109
  11.8 2.8 collective-permute-start.5
  15.1 2.8 collective-permute-start.4
  17.9 7.1 %all-to-all-done = bf16[8,24,2048]{2,1,0:T(8,128)(2,1)S(1)} async-done(((bf16[8,24,2048]{2,1,0:T(8,128)(2,1)}), bf16[8,24,2048]{2,1,0:T(8,128)(2,1)S(1)}, u32[]{:S(2)}, u32[]{:S(2)}) %all-to-all-start) | async-done | bytes 786464 | tf_op jit(solution)/shard_map/all_to_all | solution.py:109
  25.0 2.0 collective-permute-start
  27.0 2.2 collective-permute-start.1
  29.3 7.3 %collective-permute-done = bf16[80,2048]{1,0:T(8,128)(2,1)S(1)} collective-permute-done((bf16[80,2048]{1,0:T(8,128)(2,1)S(1)}, bf16[80,2048]{1,0:T(8,128)(2,1)S(1)}, u32[]{:S(2)}, u32[]{:S(2)}) %collective-permute-start) | collective-permute-done | bytes 327712 | tf_op jit(solution)/shard_map/ppermute | solution.py:18
  36.6 1.5 collective-permute-start.13
  38.3 9.9 %collective-permute-done.13 = bf16[112,2048]{1,0:T(8,128)(2,1)S(1)} collective-permute-done((bf16[112,2048]{1,0:T(8,128)(2,1)S(1)}, bf16[112,2048]{1,0:T(8,128)(2,1)S(1)}, u32[]{:S(2)}, u32[]{:S(2)}) %collective-permute-start.13) | collective-permute-done | bytes 458784 | tf_op jit(solution)/shard_map/ppermute | solution.py:22
  48.2 1.4 collective-permute-start.3
  50.4 3.1 %collective-permute-done.3 = bf16[40,2048]{1,0:T(8,128)(2,1)S(1)} collective-permute-done((bf16[40,2048]{1,0:T(8,128)(2,1)S(1)}, bf16[40,2048]{1,0:T(8,128)(2,1)S(1)}, u32[]{:S(2)}, u32[]{:S(2)}) %collective-permute-start.3) | collective-permute-done | bytes 163872 | tf_op jit(solution)/shard_map/ppermute | solution.py:18
  53.5 2.6 collective-permute-start.15
  56.2 1.6 collective-permute-start.7
  57.8 13.2 %collective-permute-done.14 = bf16[224,2048]{1,0:T(8,128)(2,1)S(1)} collective-permute-done((bf16[224,2048]{1,0:T(8,128)(2,1)S(1)}, bf16[224,2048]{1,0:T(8,128)(2,1)S(1)}, u32[]{:S(2)}, u32[]{:S(2)}) %collective-permute-start.14) | collective-permute-done | bytes 917536 | tf_op jit(solution)/shard_map/ppermute | solution.py:18
  71.2 2.7 collective-permute-done.15
  73.9 3.1 %collective-permute-start.17 = (bf16[112,2048]{1,0:T(8,128)(2,1)S(1)}, bf16[112,2048]{1,0:T(8,128)(2,1)S(1)}, u32[]{:S(2)}, u32[]{:S(2)}) collective-permute-start(bf16[112,2048]{1,0:T(8,128)(2,1)S(1)} %slice.146), channel_id=1, source_target_pairs={{0,12},{4,0},{8,4},{12,8},{1,13},{5,1},{9,5},{13,9},{2,14},{6,2},{... | collective-permute-start | bytes 1376264 | tf_op jit(solution)/shard_map/ppermute | solution.py:18
  77.2 1.8 copy-done.6
  79.0 29.8 %collective-permute-done.4 = bf16[2048,512]{1,0:T(8,128)(2,1)} collective-permute-done((bf16[2048,512]{1,0:T(8,128)(2,1)}, bf16[2048,512]{1,0:T(8,128)(2,1)}, u32[]{:S(2)}, u32[]{:S(2)}) %collective-permute-start.4) | collective-permute-done | bytes 2097184 | tf_op jit(solution)/shard_map/ppermute | solution.py:26
  108.8 7.4 %convolution_convert_fusion.2 = bf16[320,2048]{1,0:T(8,128)(2,1)} fusion(bf16[512,2048]{1,0:T(8,128)(2,1)} %collective-permute-done.6, bf16[512,2048]{1,0:T(8,128)(2,1)} %bitcast.4, bf16[320,2048]{1,0:T(8,128)(2,1)S(1)} %collective-permute-done.7, bf16[2048,512]{1,0:T(8,128)(2,1)} %collective-permute-done.4, bf16[2048,512]{1,0:T(8,128)(2,1)} %bitcast.2, ...), kind=kOutput, calls=%fused_computation.8 | convolution fusion | flops 2702770176 | bytes 11014144 | tf_op jit(solution)/shard_map/dot_general | solution.py:124
  116.2 0.8 constant_dynamic-update-slice_fusion.6
  117.0 0.8 constant_dynamic-update-slice_fusion.5
  117.8 14.0 %convolution_convert_fusion = bf16[896,2048]{1,0:T(8,128)(2,1)} fusion(f32[1024]{0:T(1024)S(1)} %pad_maximum_fusion.24, bf16[512,2048]{1,0:T(8,128)(2,1)} %collective-permute-done.6, bf16[512,2048]{1,0:T(8,128)(2,1)} %bitcast.4, bf16[896,2048]{1,0:T(8,128)(2,1)} %constant_dynamic-update-slice_fusion.5, bf16[2048,512]{1,0:T(8,128)(2,1)} %collective-permute-done.4, ...), kind=kOutput, calls=%fused_computation.3 | convolution fusion | flops 7537557504 | bytes 15732736 | tf_op jit(solution)/shard_map/dot_general | solution.py:124
  131.9 1.6 fusion.56
  133.5 4.1 %collective-permute-start.18 = (bf16[112,2048]{1,0:T(8,128)(2,1)S(1)}, bf16[112,2048]{1,0:T(8,128)(2,1)S(1)}, u32[]{:S(2)}, u32[]{:S(2)}) collective-permute-start(bf16[112,2048]{1,0:T(8,128)(2,1)S(1)} %get-tuple-element.7), channel_id=1, source_target_pairs={{0,12},{4,0},{8,4},{12,8},{1,13},{5,1},{9,5},{13,9},{2,14},{6,2},{... | collective-permute-start | bytes 1376264 | tf_op jit(solution)/shard_map/ppermute | solution.py:18
  138.1 8.7 %collective-permute-done.18 = bf16[112,2048]{1,0:T(8,128)(2,1)S(1)} collective-permute-done((bf16[112,2048]{1,0:T(8,128)(2,1)S(1)}, bf16[112,2048]{1,0:T(8,128)(2,1)S(1)}, u32[]{:S(2)}, u32[]{:S(2)}) %collective-permute-start.18) | collective-permute-done | bytes 458784 | tf_op jit(solution)/shard_map/ppermute | solution.py:18
  146.8 3.4 %collective-permute-done.20 = bf16[112,2048]{1,0:T(8,128)(2,1)S(1)} collective-permute-done((bf16[112,2048]{1,0:T(8,128)(2,1)S(1)}, bf16[112,2048]{1,0:T(8,128)(2,1)S(1)}, u32[]{:S(2)}, u32[]{:S(2)}) %collective-permute-start.20) | collective-permute-done | bytes 458784 | tf_op jit(solution)/shard_map/ppermute | solution.py:18
  150.2 1.5 add_convert_fusion.2
  151.8 7.0 %fusion = bf16[320,2048]{1,0:T(8,128)(2,1)S(1)} fusion(bf16[320,2048]{1,0:T(8,128)(2,1)} %collective-permute-done.8, bf16[512,2048]{1,0:T(8,128)(2,1)} %collective-permute-done.6, bf16[512,2048]{1,0:T(8,128)(2,1)} %bitcast.4, bf16[320,2048]{1,0:T(8,128)(2,1)} %copy-done.5, bf16[2048,512]{1,0:T(8,128)(2,1)} %collective-permute-done.4, ...), kind=kOutput, calls=%fused_computation.7 | convolution fusion | flops 2704080896 | bytes 12324864 | tf_op jit(solution)/shard_map/dot_general | solution.py:124
  159.2 1.7 collective-permute-start.11
  161.0 3.2 %collective-permute-done.9 = bf16[40,2048]{1,0:T(8,128)(2,1)S(1)} collective-permute-done((bf16[40,2048]{1,0:T(8,128)(2,1)S(1)}, bf16[40,2048]{1,0:T(8,128)(2,1)S(1)}, u32[]{:S(2)}, u32[]{:S(2)}) %collective-permute-start.9) | collective-permute-done | bytes 163872 | tf_op jit(solution)/shard_map/ppermute | solution.py:18
  164.3 2.5 collective-permute-done.11
  167.6 19.6 %collective-permute-done.21 = bf16[224,2048]{1,0:T(8,128)(2,1)S(1)} collective-permute-done((bf16[224,2048]{1,0:T(8,128)(2,1)S(1)}, bf16[224,2048]{1,0:T(8,128)(2,1)S(1)}, u32[]{:S(2)}, u32[]{:S(2)}) %collective-permute-start.21) | collective-permute-done | bytes 917536 | tf_op jit(solution)/shard_map/ppermute | solution.py:18
  187.3 1.1 collective-permute-done.19
  188.4 2.1 collective-permute-start.10
  190.5 1.6 convert_add_fusion
  192.2 4.5 %collective-permute-done.12 = bf16[80,2048]{1,0:T(8,128)(2,1)S(1)} collective-permute-done((bf16[80,2048]{1,0:T(8,128)(2,1)S(1)}, bf16[80,2048]{1,0:T(8,128)(2,1)S(1)}, u32[]{:S(2)}, u32[]{:S(2)}) %collective-permute-start.12) | collective-permute-done | bytes 327712 | tf_op jit(solution)/shard_map/ppermute | solution.py:18
  196.8 1.7 collective-permute-start.22
  198.6 8.3 %collective-permute-done.22 = bf16[112,2048]{1,0:T(8,128)(2,1)S(1)} collective-permute-done((bf16[112,2048]{1,0:T(8,128)(2,1)S(1)}, bf16[112,2048]{1,0:T(8,128)(2,1)S(1)}, u32[]{:S(2)}, u32[]{:S(2)}) %collective-permute-start.22) | collective-permute-done | bytes 458784 | tf_op jit(solution)/shard_map/ppermute | solution.py:22
  207.0 1.0 pad_maximum_fusion.15
  208.0 4.1 %all-to-all-start.1 = ((bf16[8,24,2048]{2,1,0:T(8,128)(2,1)}), bf16[8,24,2048]{2,1,0:T(8,128)(2,1)S(1)}, u32[]{:S(2)}, u32[]{:S(2)}) async-start(bf16[8,24,2048]{2,1,0:T(8,128)(2,1)} %bitcast.5), calls=%async_computation.1 | async-start | bytes 1572864 | tf_op jit(solution)/shard_map/all_to_all | solution.py:134
  212.1 4.9 %constant_dynamic-update-slice_fusion.15 = bf16[2048,2048]{1,0:T(8,128)(2,1)} fusion(bf16[1024,2048]{1,0:T(8,128)(2,1)} %param.24), kind=kLoop, calls=%fused_computation.93 | loop fusion | bytes 8388608
  217.0 2.6 constant_dynamic-update-slice_fusion.12
  219.6 5.7 %all-to-all-done.1 = bf16[8,24,2048]{2,1,0:T(8,128)(2,1)S(1)} async-done(((bf16[8,24,2048]{2,1,0:T(8,128)(2,1)}), bf16[8,24,2048]{2,1,0:T(8,128)(2,1)S(1)}, u32[]{:S(2)}, u32[]{:S(2)}) %all-to-all-start.1) | async-done | bytes 786464 | tf_op jit(solution)/shard_map/all_to_all | solution.py:134
  225.7 1.1 fusion.62
  227.3 1.2 collective-permute-start.24
  228.5 0.9 collective-permute-start.23
  229.4 4.7 %constant_dynamic-update-slice_fusion.14 = bf16[2048,2048]{1,0:T(8,128)(2,1)} fusion(bf16[2048,2048]{1,0:T(8,128)(2,1)} %constant_dynamic-update-slice_fusion.15, bf16[1024,2048]{1,0:T(8,128)(2,1)} %collective-permute-done.27), kind=kLoop, calls=%fused_computation.92 | loop fusion | bytes 8388608 | tf_op jit(solution)/shard_map/concatenate | solution.py:88
  234.1 4.7 %constant_dynamic-update-slice_fusion.11 = bf16[2048,2048]{1,0:T(8,128)(2,1)} fusion(bf16[2048,2048]{1,0:T(8,128)(2,1)} %constant_dynamic-update-slice_fusion.12, bf16[2048,1024]{1,0:T(8,128)(2,1)} %collective-permute-done.25), kind=kLoop, calls=%fused_computation.89 | loop fusion | bytes 8388608 | tf_op jit(solution)/shard_map/concatenate | solution.py:86
  238.8 2.0 collective-permute-done.24
  240.8 0.8 slice.158
  241.6 2.4 collective-permute-start.29
  244.9 12.8 %convolution_convert_fusion.1 = bf16[384,2048]{1,0:T(8,128)(2,1)S(1)} fusion(bf16[2048,2048]{1,0:T(8,128)(2,1)} %constant_dynamic-update-slice_fusion.14, bf16[2048,2048]{1,0:T(8,128)(2,1)} %constant_dynamic-update-slice_fusion.11, bf16[128,2048]{1,0:T(8,128)(2,1)} %copy-done.3, bf16[128,2048]{1,0:T(8,128)(2,1)} %copy-done.4, ...), kind=kOutput, calls=%fused_computation.5 | convolution fusion | flops 6450315264 | bytes 19931136 | tf_op jit(solution)/shard_map/dot_general | solution.py:151
  257.6 8.2 %convolution_convert_fusion.4 = bf16[128,2048]{1,0:T(8,128)(2,1)S(1)} fusion(bf16[2048,2048]{1,0:T(8,128)(2,1)} %constant_dynamic-update-slice_fusion.14, bf16[2048,2048]{1,0:T(8,128)(2,1)} %constant_dynamic-update-slice_fusion.11, bf16[64,2048]{1,0:T(8,128)(2,1)S(1)} %collective-permute-done.29, bf16[64,2048]{1,0:T(8,128)(2,1)} %collective-permute-done.28, ...), kind=kOutput, calls=%fused_computation.15 | convolution fusion | flops 2149580800 | bytes 17833984 | tf_op jit(solution)/shard_map/dot_general | solution.py:151
  265.9 3.3 %collective-permute-start.30 = (bf16[64,2048]{1,0:T(8,128)(2,1)S(1)}, bf16[64,2048]{1,0:T(8,128)(2,1)S(1)}, u32[]{:S(2)}, u32[]{:S(2)}) collective-permute-start(bf16[64,2048]{1,0:T(8,128)(2,1)S(1)} %get-tuple-element.25), channel_id=1, source_target_pairs={{0,96},{32,0},{64,32},{96,64},{1,97},{33,1},{65,33},{97,65},{2,98}... | collective-permute-start | bytes 786440 | tf_op jit(solution)/shard_map/ppermute | solution.py:18
  269.3 3.9 %collective-permute-done.30 = bf16[64,2048]{1,0:T(8,128)(2,1)S(1)} collective-permute-done((bf16[64,2048]{1,0:T(8,128)(2,1)S(1)}, bf16[64,2048]{1,0:T(8,128)(2,1)S(1)}, u32[]{:S(2)}, u32[]{:S(2)}) %collective-permute-start.30) | collective-permute-done | bytes 262176 | tf_op jit(solution)/shard_map/ppermute | solution.py:18
  273.1 3.7 %collective-permute-done.32 = bf16[64,2048]{1,0:T(8,128)(2,1)S(1)} collective-permute-done((bf16[64,2048]{1,0:T(8,128)(2,1)S(1)}, bf16[64,2048]{1,0:T(8,128)(2,1)S(1)}, u32[]{:S(2)}, u32[]{:S(2)}) %collective-permute-start.32) | collective-permute-done | bytes 262176 | tf_op jit(solution)/shard_map/ppermute | solution.py:18
  277.1 3.3 %collective-permute-start.31 = (bf16[128,2048]{1,0:T(8,128)(2,1)S(1)}, bf16[128,2048]{1,0:T(8,128)(2,1)S(1)}, u32[]{:S(2)}, u32[]{:S(2)}) collective-permute-start(bf16[128,2048]{1,0:T(8,128)(2,1)S(1)} %pad_maximum_fusion.20), channel_id=1, source_target_pairs={{0,96},{32,0},{64,32},{96,64},{1,97},{33,1},{65,33},{97,65},{2,98}... | collective-permute-start | bytes 1572872 | tf_op jit(solution)/shard_map/ppermute | solution.py:18
  280.4 8.4 %collective-permute-done.33 = bf16[128,2048]{1,0:T(8,128)(2,1)S(1)} collective-permute-done((bf16[128,2048]{1,0:T(8,128)(2,1)S(1)}, bf16[128,2048]{1,0:T(8,128)(2,1)S(1)}, u32[]{:S(2)}, u32[]{:S(2)}) %collective-permute-start.33) | collective-permute-done | bytes 524320 | tf_op jit(solution)/shard_map/ppermute | solution.py:18
  288.8 1.1 add_convert_fusion
  (96 shorter events, 6.7 us)
Async XLA Ops:
  0.0 225.6 %copy-start = (f32[8,2048]{1,0:T(8,128)S(1)}, f32[8,2048]{1,0:T(8,128)}, u32[]{:S(2)}) copy-start(f32[8,2048]{1,0:T(8,128)} %param.20) | copy-start | bytes 196612
  0.0 11.8 %copy-start.10 = (f32[1,512]{1,0:T(1,128)S(1)}, f32[1,512]{1,0:T(1,128)}, u32[]{:S(2)}) copy-start(f32[1,512]{1,0:T(1,128)} %param.18) | copy-start | bytes 6148
  7.2 17.7 %all-to-all-start = ((bf16[8,24,2048]{2,1,0:T(8,128)(2,1)}), bf16[8,24,2048]{2,1,0:T(8,128)(2,1)S(1)}, u32[]{:S(2)}, u32[]{:S(2)}) async-start(bf16[8,24,2048]{2,1,0:T(8,128)(2,1)} %bitcast), calls=%async_computation | async-start | bytes 1572864 | tf_op jit(solution)/shard_map/all_to_all | solution.py:109
  11.8 44.4 %collective-permute-start.5 = (f32[512]{0:T(512)S(1)}, f32[512]{0:T(512)S(1)}, u32[]{:S(2)}, u32[]{:S(2)}) collective-permute-start(f32[512]{0:T(512)S(1)} %bitcast.21), channel_id=1, source_target_pairs={{0,3},{3,0},{1,2},{2,1},{4,7},{7,4},{5,6},{6,5},{8,11},{11,8},{9,1... | collective-permute-start | bytes 6152 | tf_op jit(solution)/shard_map/ppermute | solution.py:26
  14.6 62.6 %collective-permute-start.6 = (bf16[512,2048]{1,0:T(8,128)(2,1)}, bf16[512,2048]{1,0:T(8,128)(2,1)}, u32[]{:S(2)}, u32[]{:S(2)}) collective-permute-start(bf16[512,2048]{1,0:T(8,128)(2,1)} %bitcast.4), channel_id=1, source_target_pairs={{0,3},{3,0},{1,2},{2,1},{4,7},{7,4},{5,6},{6,5},{8,11},{11,8},{9,1... | collective-permute-start | bytes 6291464 | tf_op jit(solution)/shard_map/ppermute | solution.py:26
  15.1 93.7 %collective-permute-start.4 = (bf16[2048,512]{1,0:T(8,128)(2,1)}, bf16[2048,512]{1,0:T(8,128)(2,1)}, u32[]{:S(2)}, u32[]{:S(2)}) collective-permute-start(bf16[2048,512]{1,0:T(8,128)(2,1)} %bitcast.2), channel_id=1, source_target_pairs={{0,3},{3,0},{1,2},{2,1},{4,7},{7,4},{5,6},{6,5},{8,11},{11,8},{9,1... | collective-permute-start | bytes 6291464 | tf_op jit(solution)/shard_map/ppermute | solution.py:26
  25.0 11.6 %collective-permute-start = (bf16[80,2048]{1,0:T(8,128)(2,1)S(1)}, bf16[80,2048]{1,0:T(8,128)(2,1)S(1)}, u32[]{:S(2)}, u32[]{:S(2)}) collective-permute-start(bf16[80,2048]{1,0:T(8,128)(2,1)S(1)} %get-tuple-element.21), channel_id=1, source_target_pairs={{0,4},{4,8},{8,12},{12,0},{1,5},{5,9},{9,13},{13,1},{2,6},{6,10},{... | collective-permute-start | bytes 983048 | tf_op jit(solution)/shard_map/ppermute | solution.py:18
  27.0 11.2 %collective-permute-start.1 = (bf16[80,2048]{1,0:T(8,128)(2,1)S(1)}, bf16[80,2048]{1,0:T(8,128)(2,1)S(1)}, u32[]{:S(2)}, u32[]{:S(2)}) collective-permute-start(bf16[80,2048]{1,0:T(8,128)(2,1)S(1)} %get-tuple-element.21), channel_id=1, source_target_pairs={{0,12},{4,0},{8,4},{12,8},{1,13},{5,1},{9,5},{13,9},{2,14},{6,2},{... | collective-permute-start | bytes 983048 | tf_op jit(solution)/shard_map/ppermute | solution.py:18
  36.6 11.6 %collective-permute-start.13 = (bf16[112,2048]{1,0:T(8,128)(2,1)S(1)}, bf16[112,2048]{1,0:T(8,128)(2,1)S(1)}, u32[]{:S(2)}, u32[]{:S(2)}) collective-permute-start(bf16[112,2048]{1,0:T(8,128)(2,1)S(1)} %get-tuple-element.23), channel_id=1, source_target_pairs={{0,1},{1,0},{2,3},{3,2},{4,5},{5,4},{6,7},{7,6},{8,9},{9,8},{10,11... | collective-permute-start | bytes 1376264 | tf_op jit(solution)/shard_map/ppermute | solution.py:22
  38.2 11.6 %collective-permute-start.2 = (bf16[40,2048]{1,0:T(8,128)(2,1)S(1)}, bf16[40,2048]{1,0:T(8,128)(2,1)S(1)}, u32[]{:S(2)}, u32[]{:S(2)}) collective-permute-start(bf16[40,2048]{1,0:T(8,128)(2,1)S(1)} %slice.136), channel_id=1, source_target_pairs={{0,4},{4,8},{8,12},{12,0},{1,5},{5,9},{9,13},{13,1},{2,6},{6,10},{... | collective-permute-start | bytes 491528 | tf_op jit(solution)/shard_map/ppermute | solution.py:18
  48.2 5.3 %collective-permute-start.3 = (bf16[40,2048]{1,0:T(8,128)(2,1)S(1)}, bf16[40,2048]{1,0:T(8,128)(2,1)S(1)}, u32[]{:S(2)}, u32[]{:S(2)}) collective-permute-start(bf16[40,2048]{1,0:T(8,128)(2,1)S(1)} %slice.137), channel_id=1, source_target_pairs={{0,12},{4,0},{8,4},{12,8},{1,13},{5,1},{9,5},{13,9},{2,14},{6,2},{... | collective-permute-start | bytes 491528 | tf_op jit(solution)/shard_map/ppermute | solution.py:18
  49.8 21.3 %collective-permute-start.14 = (bf16[224,2048]{1,0:T(8,128)(2,1)S(1)}, bf16[224,2048]{1,0:T(8,128)(2,1)S(1)}, u32[]{:S(2)}, u32[]{:S(2)}) collective-permute-start(bf16[224,2048]{1,0:T(8,128)(2,1)S(1)} %pad_maximum_fusion.12), channel_id=1, source_target_pairs={{0,4},{4,8},{8,12},{12,0},{1,5},{5,9},{9,13},{13,1},{2,6},{6,10},{... | collective-permute-start | bytes 2752520 | tf_op jit(solution)/shard_map/ppermute | solution.py:18
  53.5 20.3 %collective-permute-start.15 = (bf16[224,2048]{1,0:T(8,128)(2,1)S(1)}, bf16[224,2048]{1,0:T(8,128)(2,1)S(1)}, u32[]{:S(2)}, u32[]{:S(2)}) collective-permute-start(bf16[224,2048]{1,0:T(8,128)(2,1)S(1)} %pad_maximum_fusion.12), channel_id=1, source_target_pairs={{0,12},{4,0},{8,4},{12,8},{1,13},{5,1},{9,5},{13,9},{2,14},{6,2},{... | collective-permute-start | bytes 2752520 | tf_op jit(solution)/shard_map/ppermute | solution.py:18
  56.2 21.0 %copy-start.5 = (bf16[320,2048]{1,0:T(8,128)(2,1)}, bf16[320,2048]{1,0:T(8,128)(2,1)S(1)}, u32[]{:S(2)}) copy-start(bf16[320,2048]{1,0:T(8,128)(2,1)S(1)} %constant_dynamic-update-slice_fusion) | copy-start | bytes 3932164
  56.2 52.6 %collective-permute-start.7 = (bf16[320,2048]{1,0:T(8,128)(2,1)S(1)}, bf16[320,2048]{1,0:T(8,128)(2,1)S(1)}, u32[]{:S(2)}, u32[]{:S(2)}) collective-permute-start(bf16[320,2048]{1,0:T(8,128)(2,1)S(1)} %constant_dynamic-update-slice_fusion), channel_id=1, source_target_pairs={{0,1},{1,0},{2,3},{3,2},{4,5},{5,4},{6,7},{7,6},{8,9},{9,8},{10,11... | collective-permute-start | bytes 3932168 | tf_op jit(solution)/shard_map/ppermute | solution.py:22
  71.1 45.1 %collective-permute-start.16 = (bf16[112,2048]{1,0:T(8,128)(2,1)S(1)}, bf16[112,2048]{1,0:T(8,128)(2,1)S(1)}, u32[]{:S(2)}, u32[]{:S(2)}) collective-permute-start(bf16[112,2048]{1,0:T(8,128)(2,1)S(1)} %slice.145), channel_id=1, source_target_pairs={{0,4},{4,8},{8,12},{12,0},{1,5},{5,9},{9,13},{13,1},{2,6},{6,10},{... | collective-permute-start | bytes 1376264 | tf_op jit(solution)/shard_map/ppermute | solution.py:18
  73.9 43.1 %collective-permute-start.17 = (bf16[112,2048]{1,0:T(8,128)(2,1)S(1)}, bf16[112,2048]{1,0:T(8,128)(2,1)S(1)}, u32[]{:S(2)}, u32[]{:S(2)}) collective-permute-start(bf16[112,2048]{1,0:T(8,128)(2,1)S(1)} %slice.146), channel_id=1, source_target_pairs={{0,12},{4,0},{8,4},{12,8},{1,13},{5,1},{9,5},{13,9},{2,14},{6,2},{... | collective-permute-start | bytes 1376264 | tf_op jit(solution)/shard_map/ppermute | solution.py:18
  77.2 1.8 copy-start.6
  116.2 35.5 %collective-permute-start.8 = (bf16[320,2048]{1,0:T(8,128)(2,1)}, bf16[320,2048]{1,0:T(8,128)(2,1)}, u32[]{:S(2)}, u32[]{:S(2)}) collective-permute-start(bf16[320,2048]{1,0:T(8,128)(2,1)} %convolution_convert_fusion.2), channel_id=1, source_target_pairs={{0,1},{1,0},{2,3},{3,2},{4,5},{5,4},{6,7},{7,6},{8,9},{9,8},{10,11... | collective-permute-start | bytes 3932168 | tf_op jit(solution)/shard_map/ppermute | solution.py:22
  131.9 14.9 %copy-start.9 = (f32[1024]{0:T(1024)S(1)}, f32[1024]{0:T(1024)}, u32[]{:S(2)}) copy-start(f32[1024]{0:T(1024)} %param.23) | copy-start | bytes 12292
  133.5 13.4 %collective-permute-start.18 = (bf16[112,2048]{1,0:T(8,128)(2,1)S(1)}, bf16[112,2048]{1,0:T(8,128)(2,1)S(1)}, u32[]{:S(2)}, u32[]{:S(2)}) collective-permute-start(bf16[112,2048]{1,0:T(8,128)(2,1)S(1)} %get-tuple-element.7), channel_id=1, source_target_pairs={{0,12},{4,0},{8,4},{12,8},{1,13},{5,1},{9,5},{13,9},{2,14},{6,2},{... | collective-permute-start | bytes 1376264 | tf_op jit(solution)/shard_map/ppermute | solution.py:18
  137.6 12.7 %collective-permute-start.20 = (bf16[112,2048]{1,0:T(8,128)(2,1)S(1)}, bf16[112,2048]{1,0:T(8,128)(2,1)S(1)}, u32[]{:S(2)}, u32[]{:S(2)}) collective-permute-start(bf16[112,2048]{1,0:T(8,128)(2,1)S(1)} %get-tuple-element.8), channel_id=1, source_target_pairs={{0,4},{4,8},{8,12},{12,0},{1,5},{5,9},{9,13},{13,1},{2,6},{6,10},{... | collective-permute-start | bytes 1376264 | tf_op jit(solution)/shard_map/ppermute | solution.py:18
  137.6 91.8 %collective-permute-start.27 = (bf16[1024,2048]{1,0:T(8,128)(2,1)}, bf16[1024,2048]{1,0:T(8,128)(2,1)}, u32[]{:S(2)}, u32[]{:S(2)}) collective-permute-start(bf16[1024,2048]{1,0:T(8,128)(2,1)} %param.24), channel_id=1, source_target_pairs={{0,16},{16,0},{1,17},{17,1},{2,18},{18,2},{3,19},{19,3},{4,20},{20... | collective-permute-start | bytes 12582920 | tf_op jit(solution)/shard_map/ppermute | solution.py:30
  137.6 96.5 %collective-permute-start.25 = (bf16[2048,1024]{1,0:T(8,128)(2,1)}, bf16[2048,1024]{1,0:T(8,128)(2,1)}, u32[]{:S(2)}, u32[]{:S(2)}) collective-permute-start(bf16[2048,1024]{1,0:T(8,128)(2,1)} %param.22), channel_id=1, source_target_pairs={{0,16},{16,0},{1,17},{17,1},{2,18},{18,2},{3,19},{19,3},{4,20},{20... | collective-permute-start | bytes 12582920 | tf_op jit(solution)/shard_map/ppermute | solution.py:30
  146.8 72.8 %collective-permute-start.26 = (f32[1024]{0:T(1024)S(1)}, f32[1024]{0:T(1024)S(1)}, u32[]{:S(2)}, u32[]{:S(2)}) collective-permute-start(f32[1024]{0:T(1024)S(1)} %copy-done.9), channel_id=1, source_target_pairs={{0,16},{16,0},{1,17},{17,1},{2,18},{18,2},{3,19},{19,3},{4,20},{20... | collective-permute-start | bytes 12296 | tf_op jit(solution)/shard_map/ppermute | solution.py:30
  158.9 5.4 %collective-permute-start.9 = (bf16[40,2048]{1,0:T(8,128)(2,1)S(1)}, bf16[40,2048]{1,0:T(8,128)(2,1)S(1)}, u32[]{:S(2)}, u32[]{:S(2)}) collective-permute-start(bf16[40,2048]{1,0:T(8,128)(2,1)S(1)} %get-tuple-element.17), channel_id=1, source_target_pairs={{0,12},{4,0},{8,4},{12,8},{1,13},{5,1},{9,5},{13,9},{2,14},{6,2},{... | collective-permute-start | bytes 491528 | tf_op jit(solution)/shard_map/ppermute | solution.py:18
  159.2 7.5 %collective-permute-start.11 = (bf16[40,2048]{1,0:T(8,128)(2,1)S(1)}, bf16[40,2048]{1,0:T(8,128)(2,1)S(1)}, u32[]{:S(2)}, u32[]{:S(2)}) collective-permute-start(bf16[40,2048]{1,0:T(8,128)(2,1)S(1)} %get-tuple-element.18), channel_id=1, source_target_pairs={{0,4},{4,8},{8,12},{12,0},{1,5},{5,9},{9,13},{13,1},{2,6},{6,10},{... | collective-permute-start | bytes 491528 | tf_op jit(solution)/shard_map/ppermute | solution.py:18
  164.3 23.0 %collective-permute-start.21 = (bf16[224,2048]{1,0:T(8,128)(2,1)S(1)}, bf16[224,2048]{1,0:T(8,128)(2,1)S(1)}, u32[]{:S(2)}, u32[]{:S(2)}) collective-permute-start(bf16[224,2048]{1,0:T(8,128)(2,1)S(1)} %pad_maximum_fusion.14), channel_id=1, source_target_pairs={{0,4},{4,8},{8,12},{12,0},{1,5},{5,9},{9,13},{13,1},{2,6},{6,10},{... | collective-permute-start | bytes 2752520 | tf_op jit(solution)/shard_map/ppermute | solution.py:18
  166.8 21.7 %collective-permute-start.19 = (bf16[224,2048]{1,0:T(8,128)(2,1)S(1)}, bf16[224,2048]{1,0:T(8,128)(2,1)S(1)}, u32[]{:S(2)}, u32[]{:S(2)}) collective-permute-start(bf16[224,2048]{1,0:T(8,128)(2,1)S(1)} %pad_maximum_fusion.13), channel_id=1, source_target_pairs={{0,12},{4,0},{8,4},{12,8},{1,13},{5,1},{9,5},{13,9},{2,14},{6,2},{... | collective-permute-start | bytes 2752520 | tf_op jit(solution)/shard_map/ppermute | solution.py:18
  187.3 9.5 %collective-permute-start.12 = (bf16[80,2048]{1,0:T(8,128)(2,1)S(1)}, bf16[80,2048]{1,0:T(8,128)(2,1)S(1)}, u32[]{:S(2)}, u32[]{:S(2)}) collective-permute-start(bf16[80,2048]{1,0:T(8,128)(2,1)S(1)} %pad_maximum_fusion.23), channel_id=1, source_target_pairs={{0,4},{4,8},{8,12},{12,0},{1,5},{5,9},{9,13},{13,1},{2,6},{6,10},{... | collective-permute-start | bytes 983048 | tf_op jit(solution)/shard_map/ppermute | solution.py:18
  188.4 10.1 %collective-permute-start.10 = (bf16[80,2048]{1,0:T(8,128)(2,1)S(1)}, bf16[80,2048]{1,0:T(8,128)(2,1)S(1)}, u32[]{:S(2)}, u32[]{:S(2)}) collective-permute-start(bf16[80,2048]{1,0:T(8,128)(2,1)S(1)} %pad_maximum_fusion.22), channel_id=1, source_target_pairs={{0,12},{4,0},{8,4},{12,8},{1,13},{5,1},{9,5},{13,9},{2,14},{6,2},{... | collective-permute-start | bytes 983048 | tf_op jit(solution)/shard_map/ppermute | solution.py:18
  196.8 10.1 %collective-permute-start.22 = (bf16[112,2048]{1,0:T(8,128)(2,1)S(1)}, bf16[112,2048]{1,0:T(8,128)(2,1)S(1)}, u32[]{:S(2)}, u32[]{:S(2)}) collective-permute-start(bf16[112,2048]{1,0:T(8,128)(2,1)S(1)} %slice.177), channel_id=1, source_target_pairs={{0,1},{1,0},{2,3},{3,2},{4,5},{5,4},{6,7},{7,6},{8,9},{9,8},{10,11... | collective-permute-start | bytes 1376264 | tf_op jit(solution)/shard_map/ppermute | solution.py:22
  208.0 17.3 %all-to-all-start.1 = ((bf16[8,24,2048]{2,1,0:T(8,128)(2,1)}), bf16[8,24,2048]{2,1,0:T(8,128)(2,1)S(1)}, u32[]{:S(2)}, u32[]{:S(2)}) async-start(bf16[8,24,2048]{2,1,0:T(8,128)(2,1)} %bitcast.5), calls=%async_computation.1 | async-start | bytes 1572864 | tf_op jit(solution)/shard_map/all_to_all | solution.py:134
  212.1 4.9 %copy-start.2 = (bf16[2048,1024]{1,0:T(8,128)(2,1)S(1)}, bf16[2048,1024]{1,0:T(8,128)(2,1)}, u32[]{:S(2)}) copy-start(bf16[2048,1024]{1,0:T(8,128)(2,1)} %param.22) | copy-start | bytes 12582916
  217.0 8.2 %copy-start.1 = (bf16[128,2048]{1,0:T(8,128)(2,1)S(1)}, bf16[128,2048]{1,0:T(8,128)(2,1)}, u32[]{:S(2)}) copy-start(bf16[128,2048]{1,0:T(8,128)(2,1)} %param.13) | copy-start | bytes 1572868
  219.6 7.5 %copy-start.7 = (f32[2048]{0:T(1024)S(1)}, f32[2048]{0:T(1024)}, u32[]{:S(2)}) copy-start(f32[2048]{0:T(1024)} %param.21) | copy-start | bytes 24580
  227.3 13.5 %collective-permute-start.24 = (bf16[128,2048]{1,0:T(8,128)(2,1)S(1)}, bf16[128,2048]{1,0:T(8,128)(2,1)S(1)}, u32[]{:S(2)}, u32[]{:S(2)}) collective-permute-start(bf16[128,2048]{1,0:T(8,128)(2,1)S(1)} %multiply_convert_fusion), channel_id=1, source_target_pairs={{0,96},{32,0},{64,32},{96,64},{1,97},{33,1},{65,33},{97,65},{2,98}... | collective-permute-start | bytes 1572872 | tf_op jit(solution)/shard_map/ppermute | solution.py:18
  228.5 15.4 %collective-permute-start.23 = (bf16[128,2048]{1,0:T(8,128)(2,1)S(1)}, bf16[128,2048]{1,0:T(8,128)(2,1)S(1)}, u32[]{:S(2)}, u32[]{:S(2)}) collective-permute-start(bf16[128,2048]{1,0:T(8,128)(2,1)S(1)} %multiply_convert_fusion), channel_id=1, source_target_pairs={{0,32},{32,64},{64,96},{96,0},{1,33},{33,65},{65,97},{97,1},{2,34}... | collective-permute-start | bytes 1572872 | tf_op jit(solution)/shard_map/ppermute | solution.py:18
  240.8 3.9 %copy-start.3 = (bf16[128,2048]{1,0:T(8,128)(2,1)}, bf16[128,2048]{1,0:T(8,128)(2,1)S(1)}, u32[]{:S(2)}) copy-start(bf16[128,2048]{1,0:T(8,128)(2,1)S(1)} %collective-permute-done.24) | copy-start | bytes 1572868
  241.6 16.0 %collective-permute-start.29 = (bf16[64,2048]{1,0:T(8,128)(2,1)}, bf16[64,2048]{1,0:T(8,128)(2,1)S(1)}, u32[]{:S(2)}, u32[]{:S(2)}) collective-permute-start(bf16[64,2048]{1,0:T(8,128)(2,1)} %slice.158), channel_id=1, source_target_pairs={{0,96},{32,0},{64,32},{96,64},{1,97},{33,1},{65,33},{97,65},{2,98}... | collective-permute-start | bytes 786440 | tf_op jit(solution)/shard_map/ppermute | solution.py:18
  244.0 0.9 copy-start.4
  244.9 12.8 %collective-permute-start.28 = (bf16[64,2048]{1,0:T(8,128)(2,1)}, bf16[64,2048]{1,0:T(8,128)(2,1)}, u32[]{:S(2)}, u32[]{:S(2)}) collective-permute-start(bf16[64,2048]{1,0:T(8,128)(2,1)} %slice.157), channel_id=1, source_target_pairs={{0,32},{32,64},{64,96},{96,0},{1,33},{33,65},{65,97},{97,1},{2,34}... | collective-permute-start | bytes 786440 | tf_op jit(solution)/shard_map/ppermute | solution.py:18
  265.9 23.0 %copy-start.8 = (f32[2048]{0:T(1024)S(1)}, f32[2048]{0:T(1024)}, u32[]{:S(2)}) copy-start(f32[2048]{0:T(1024)} %param.25) | copy-start | bytes 24580
  265.9 7.2 %collective-permute-start.30 = (bf16[64,2048]{1,0:T(8,128)(2,1)S(1)}, bf16[64,2048]{1,0:T(8,128)(2,1)S(1)}, u32[]{:S(2)}, u32[]{:S(2)}) collective-permute-start(bf16[64,2048]{1,0:T(8,128)(2,1)S(1)} %get-tuple-element.25), channel_id=1, source_target_pairs={{0,96},{32,0},{64,32},{96,64},{1,97},{33,1},{65,33},{97,65},{2,98}... | collective-permute-start | bytes 786440 | tf_op jit(solution)/shard_map/ppermute | solution.py:18
  269.2 7.6 %collective-permute-start.32 = (bf16[64,2048]{1,0:T(8,128)(2,1)S(1)}, bf16[64,2048]{1,0:T(8,128)(2,1)S(1)}, u32[]{:S(2)}, u32[]{:S(2)}) collective-permute-start(bf16[64,2048]{1,0:T(8,128)(2,1)S(1)} %get-tuple-element.26), channel_id=1, source_target_pairs={{0,32},{32,64},{64,96},{96,0},{1,33},{33,65},{65,97},{97,1},{2,34}... | collective-permute-start | bytes 786440 | tf_op jit(solution)/shard_map/ppermute | solution.py:18
  277.0 11.9 %collective-permute-start.33 = (bf16[128,2048]{1,0:T(8,128)(2,1)S(1)}, bf16[128,2048]{1,0:T(8,128)(2,1)S(1)}, u32[]{:S(2)}, u32[]{:S(2)}) collective-permute-start(bf16[128,2048]{1,0:T(8,128)(2,1)S(1)} %pad_maximum_fusion.21), channel_id=1, source_target_pairs={{0,32},{32,64},{64,96},{96,0},{1,33},{33,65},{65,97},{97,1},{2,34}... | collective-permute-start | bytes 1572872 | tf_op jit(solution)/shard_map/ppermute | solution.py:18
  277.1 11.7 %collective-permute-start.31 = (bf16[128,2048]{1,0:T(8,128)(2,1)S(1)}, bf16[128,2048]{1,0:T(8,128)(2,1)S(1)}, u32[]{:S(2)}, u32[]{:S(2)}) collective-permute-start(bf16[128,2048]{1,0:T(8,128)(2,1)S(1)} %pad_maximum_fusion.20), channel_id=1, source_target_pairs={{0,96},{32,0},{64,32},{96,64},{1,97},{33,1},{65,33},{97,65},{2,98}... | collective-permute-start | bytes 1572872 | tf_op jit(solution)/shard_map/ppermute | solution.py:18
